TPU v7x, 256 devices: a whole 4x4x8 slice. The times are simulated.
256 devices in a mesh: blk: 64 (over z, x, y_hi), slab: 4 (over y_lo, core).
Axes of the slice: x: 4, y: 4 (y_hi: 2, y_lo: 2; y = y_hi * 2 + y_lo), z: 8, core: 2. Of those that a mesh axis runs over, the one named last changes fastest.
Arguments:
- a_tiles: bfloat16 [32768, 8192], P('blk', 'slab'), may hold values from -0.125 to 0.125
- tile_cols: int32 [128, 4, 8], P('blk', 'slab'), may hold values from 0 to 15, as said below
- tile_counts: int32 [128, 4], P('blk', 'slab'), may hold values from 1 to 8, as said below
- scaling: float32 [16384], P('slab'), may hold values from 0.1 to 10
- panel: int32 [1], replicated, may hold values from 0 to 127
Outputs:
- normal_band: float32 [32768, 3, 512], P('blk', None, 'slab')
Inputs may be any that keep to these rules, and one draw needn't show every extreme that they name: `tile_cols`: the 8 column tiles listed for one row block in one slab are distinct. `tile_counts`: the largest count is 8 in every draw.
All inputs are finite; a program needn't handle non-finite values.
Results may differ from a plain program's by a relative error of at most 0.0015.
Values may be sent and summed in bfloat16 or wider, within the bound.
No kernel may reach another device: no remote copies, remote signals or barrier semaphores. Data moves between devices by JAX's collectives and lax.ppermute only.
A program may use at most 64 MiB of HBM per device.

v0:
```python
import jax
import jax.numpy as jnp
from jax import lax
from jax.experimental import pallas as pl
from jax.experimental.pallas import tpu as pltpu
from jax.sharding import PartitionSpec as P

ridge_shift = 0.05
AXES = ("blk", "slab")
HIGH = lax.Precision.HIGHEST
SMEM = pl.BlockSpec(memory_space=pltpu.SMEM)
ANY = pl.BlockSpec(memory_space=pl.ANY)
VMEM = pl.BlockSpec(memory_space=pltpu.VMEM)


def product(lhs, rhs, lhs_cols, rhs_cols, scaling, table, scaled, tile, slots, col_tiles, emit):
    for b in range(2):
        for c in range(col_tiles):
            table[b, c] = jnp.int32(slots)
    for b in range(2):
        for n in range(slots):
            col = rhs_cols[b, n]
            table[b, col] = jnp.int32(n)

    def left(t, carry):
        i = t // slots
        m = t % slots
        col = lhs_cols[i, m]
        live = col < col_tiles
        col = jnp.minimum(col, col_tiles - 1)
        other = [table[b, col] for b in range(2)]

        @pl.when(live & ((other[0] < slots) | (other[1] < slots)))
        def _():
            rows = pl.ds(pl.multiple_of(i * tile, tile), tile)
            cols = pl.ds(pl.multiple_of(m * tile, tile), tile)
            scaled[...] = (lhs[rows, cols].astype(jnp.float32) * scaling[pl.ds(col, 1), :]).astype(jnp.bfloat16)
            for b in range(2):

                @pl.when(other[b] < slots)
                def _():
                    cols = pl.ds(pl.multiple_of(other[b] * tile, tile), tile)
                    emit(i, b, lax.dot_general(
                        scaled[...], rhs[b * tile:(b + 1) * tile, cols],
                        (((1,), (1,)), ((), ())), preferred_element_type=jnp.float32))

        return carry

    lax.fori_loop(0, 2 * slots, left, 0)


def live_cols(tile_cols, tile_counts, cols, slots, col_tiles):
    for b in range(2):
        for n in range(slots):
            cols[b, n] = jnp.where(n < tile_counts[b], tile_cols[b, 0, n], col_tiles)


def pack_kernel(slots, col_tiles, tile_cols, tile_counts, a, out, held, cols, tail, sems):
    pieces = 4
    rows = a.shape[0]
    size = rows // pieces
    part = [pl.ds(p * size, size) for p in range(pieces)]
    reads = [pltpu.make_async_copy(a.at[part[p], :], held.at[part[p], :], sems.at[p]) for p in range(pieces)]
    writes = [pltpu.make_async_copy(held.at[part[p], :], out.at[part[p], :], sems.at[pieces + p]) for p in range(pieces)]
    for copy in reads:
        copy.start()
    live_cols(tile_cols, tile_counts, cols, slots, col_tiles)
    row = lax.broadcasted_iota(jnp.int32, tail.shape, 0)
    lane = lax.broadcasted_iota(jnp.int32, tail.shape, 1)
    value = jnp.zeros(tail.shape, jnp.float32)
    for b in range(2):
        for n in range(slots):
            value = jnp.where((row == b) & (lane == n), cols[b, n].astype(jnp.float32), value)
    tail[...] = value.astype(tail.dtype)
    last = pltpu.make_async_copy(
        tail, out.at[pl.ds(rows, tail.shape[0]), pl.ds(0, tail.shape[1])], sems.at[2 * pieces])
    last.start()
    for read, write in zip(reads, writes):
        read.wait()
        write.start()
    for write in writes:
        write.wait()
    last.wait()


def tail_cols(packed, rows, tails, ints, cols, sems, first):
    count = len(packed)
    lists = [pltpu.make_async_copy(
        packed[n].at[pl.ds(rows, tails.shape[1]), pl.ds(0, tails.shape[2])], tails.at[n], sems.at[first + n])
        for n in range(count)]
    for copy in lists:
        copy.start()

    def finish():
        scalars = [pltpu.make_async_copy(ints.at[n], cols[n], sems.at[first + count + n]) for n in range(count)]
        for n in range(count):
            lists[n].wait()
            ints[n] = tails[n].astype(jnp.float32)[:ints.shape[1]].astype(jnp.int32)
            scalars[n].start()
        for copy in scalars:
            copy.wait()

    return finish


def own_kernel(tile, slots, col_tiles, tile_cols, tile_counts, scaling, a, give, keep, cols, table, scaled, acc):
    slab = lax.axis_index("slab")
    core = slab % 2
    y_lo = slab // 2
    rows = acc.shape[1]
    acc[...] = jnp.zeros_like(acc)
    live_cols(tile_cols, tile_counts, cols, slots, col_tiles)

    def emit(i, b, value):
        acc[b, pl.ds(pl.multiple_of(i * tile, tile), tile), :] += value

    product(a, a, cols, cols, scaling, table, scaled, tile, slots, col_tiles, emit)
    give[:rows, :] = acc[y_lo]
    keep[:rows, :] = acc[y_lo]
    give[rows:, :] = acc[1 - y_lo, pl.ds(pl.multiple_of((1 - core) * tile, tile), tile), :]
    keep[rows:, :] = acc[1 - y_lo, pl.ds(pl.multiple_of(core * tile, tile), tile), :]


def fetch(copies, sems):
    started = [pltpu.make_async_copy(src, dst, sems.at[n]) for n, (src, dst) in enumerate(copies)]
    for copy in started:
        copy.start()
    return started


def adder(acc, tile):
    half = tile // 2

    def emit(i, b, value):
        at = pl.ds(pl.multiple_of(i * tile, tile), tile)
        acc[2 * b, at, :] += value[:, :half]
        acc[2 * b + 1, at, :] += value[:, half:]

    return emit


def second_kernel(tile, slots, col_tiles, tile_cols, tile_counts, scaling, a_any, x_any, p1, p2, p3, kept,
                  a, x, cols, x_cols, tail, ints, table, scaled, acc, sems):
    slab = lax.axis_index("slab")
    core = slab % 2
    rows = a.shape[0]
    finish = tail_cols([x_any], rows, tail, ints, [x_cols], sems, 2)
    copies = fetch([(a_any, a), (x_any.at[pl.ds(0, rows), :], x)], sems)
    args = (scaling, table, scaled, tile, slots, col_tiles, adder(acc, tile))
    finish()
    live_cols(tile_cols, tile_counts, cols, slots, col_tiles)
    acc[...] = jnp.zeros_like(acc)
    for copy in copies:
        copy.wait()

    @pl.when(core == 0)
    def _():
        product(a, x, cols, x_cols, *args)

    @pl.when(core == 1)
    def _():
        product(x, a, x_cols, cols, *args)

    kept[...] = acc[slab]
    for k, ref in ((1, p1), (2, p2), (3, p3)):
        ref[...] = acc[slab ^ k].astype(ref.dtype)


def first_kernel(tile, slots, col_tiles, tile_cols, tile_counts, scaling, a_any, x_any, y_any, q1, q2, q3, kept,
                 a, x, y, cols, x_cols, y_cols, tail, ints, table, scaled, acc, sems):
    slab = lax.axis_index("slab")
    core = slab % 2
    hub = (core + lax.axis_index("blk")) % 2 == 1
    rows = a.shape[0]

    def store(start):
        kept[start:start + rows, :] = acc[slab]
        for k, ref in ((1, q1), (2, q2), (3, q3)):
            ref[start:start + rows, :] = acc[slab ^ k].astype(ref.dtype)

    @pl.when(jnp.logical_not(hub))
    def _():
        kept[...] = jnp.zeros_like(kept)

    @pl.when(hub)
    def _():
        part = pl.ds(0, rows)
        finish = tail_cols([x_any, y_any], rows, tail, ints, [x_cols, y_cols], sems, 3)
        y_copy = pltpu.make_async_copy(y_any.at[part, :], y, sems.at[0])
        x_copy = pltpu.make_async_copy(x_any.at[part, :], x, sems.at[1])
        a_copy = pltpu.make_async_copy(a_any, a, sems.at[2])
        y_copy.start()

        @pl.when(core == 0)
        def _():
            x_copy.start()
            a_copy.start()

        @pl.when(core == 1)
        def _():
            a_copy.start()
            x_copy.start()

        finish()
        live_cols(tile_cols, tile_counts, cols, slots, col_tiles)
        args = (scaling, table, scaled, tile, slots, col_tiles, adder(acc, tile))
        acc[...] = jnp.zeros_like(acc)
        y_copy.wait()

        @pl.when(core == 0)
        def _():
            x_copy.wait()
            product(y, x, y_cols, x_cols, *args)

        @pl.when(core == 1)
        def _():
            a_copy.wait()
            product(y, a, y_cols, cols, *args)

        store(0)
        acc[...] = jnp.zeros_like(acc)

        @pl.when(core == 0)
        def _():
            a_copy.wait()
            product(a, y, cols, y_cols, *args)

        @pl.when(core == 1)
        def _():
            x_copy.wait()
            product(x, y, x_cols, y_cols, *args)

        store(rows)


def eliminate(matrix, size, group):
    tiles = size // 8
    v = matrix.reshape(tiles, 8, 128)
    ids = lax.broadcasted_iota(jnp.int32, (tiles, 8, 128), 0) * 8 + lax.broadcasted_iota(
        jnp.int32, (tiles, 8, 128), 1)
    pivots = [jnp.ones((8, 128), jnp.float32) for _ in range(tiles)]
    for j in range(0, size, group):
        s = {}
        for a in range(group):
            for b in range(a + 1):
                r = j + a
                s[a, b] = jnp.broadcast_to(v[r // 8, r % 8:r % 8 + 1, j + b:j + b + 1], (8, 128))
        rows = [jnp.broadcast_to(v[(j + a) // 8, (j + a) % 8:(j + a) % 8 + 1, :], (8, 128)) for a in range(group)]
        below = (j + group) // 8
        last = j + group >= size
        cols = [] if last else [
            jnp.broadcast_to(v[below:, :, j + b:j + b + 1], (tiles - below, 8, 128)) for b in range(group)]
        low = {}
        inverse = []
        for b in range(group):
            inverse.append(1.0 / s[b, b])
            for a in range(b + 1, group):
                low[a, b] = s[a, b] * inverse[b]
            for a in range(b + 1, group):
                for c in range(b + 1, a + 1):
                    s[a, c] = s[a, c] - low[a, b] * s[c, b]
        for a in range(group):
            for b in range(a):
                rows[a] = rows[a] - low[a, b] * rows[b]
        top = j // 8
        kept = v[top]
        for a in range(group):
            here = ids[top] == j + a
            kept = jnp.where(here, rows[a], kept)
            pivots[top] = jnp.where(here, s[a, a], pivots[top])
        pieces = [v[:top]] if top else []
        pieces.append(kept[None])
        if not last:
            steps = []
            update = None
            for b in range(group):
                step = cols[b]
                for k in range(b):
                    step = step - steps[k] * s[b, k][None]
                steps.append(step * inverse[b][None])
                term = steps[b] * rows[b][None]
                update = term if update is None else update + term
            pieces.append(v[below:] - update)
        v = jnp.concatenate(pieces, 0) if len(pieces) > 1 else pieces[0]
    return (v * lax.rsqrt(jnp.stack(pivots))).reshape(size, 128)


def panel_factor(w, u, first, stop, size, group):
    n, width = w.shape
    for start in range(first, stop, size):
        base = start // 128 * 128
        square = w[start:start + size, base:base + 128]
        if start > base:
            square = pltpu.roll(square, 128 - (start - base), 1)
        lane = lax.broadcasted_iota(jnp.int32, (size, 128), 1)
        row = lax.broadcasted_iota(jnp.int32, (size, 128), 0)
        square = jnp.where(lane < size, square, jnp.where(lane - size == row, 1.0, 0.0))
        inverse = eliminate(square, size, group)[:, size:2 * size]
        strip = lax.dot_general(
            inverse, w[start:start + size, :], (((1,), (0,)), ((), ())),
            precision=HIGH, preferred_element_type=jnp.float32)
        lane = lax.broadcasted_iota(jnp.int32, (size, width), 1)
        row = lax.broadcasted_iota(jnp.int32, (size, width), 0)
        strip = jnp.where(lane - start >= row, strip, 0.0)
        u[start:start + size, :] = strip
        if start + size < n:
            w[start + size:, :] = w[start + size:, :] - lax.dot_general(
                strip[:, start + size:n], strip, (((0,), (0,)), ((), ())),
                precision=HIGH, preferred_element_type=jnp.float32)


def holds_panel(panel):
    block = panel[0]
    pos = block % 2
    return (block // 2 == lax.axis_index("blk")) & (pos == lax.axis_index("slab") // 2), pos


def panel_head(tile, panel, keep, got, mine, theirs, column, top, rest, total, w, u, sems):
    slab = lax.axis_index("slab")
    core = slab % 2
    y_lo = slab // 2
    half = tile // 2
    holds, pos = holds_panel(panel)
    rows = total.shape[0]
    total[...] = keep[:rows, :] + got[:rows, :]
    total[pl.ds(pl.multiple_of(core * tile, tile), tile), :] += mine[...]
    total[pl.ds(pl.multiple_of((1 - core) * tile, tile), tile), :] += theirs[...]
    eye = jnp.where(
        lax.broadcasted_iota(jnp.int32, (tile, tile), 0) == lax.broadcasted_iota(jnp.int32, (tile, tile), 1),
        jnp.float32(ridge_shift), jnp.float32(0.0))
    total[pl.ds(pl.multiple_of(y_lo * tile, tile), tile), :] += eye

    @pl.when(core == 0)
    def _():
        column[...] = total[:, :half]

    @pl.when(core == 1)
    def _():
        column[...] = total[:, half:]

    @pl.when(holds)
    def _():
        square = total[pl.ds(pl.multiple_of(pos * tile, tile), tile), :]
        w[:, :tile] = (square + square.T) * 0.5
        w[:, tile:] = total[pl.ds(pl.multiple_of((1 - pos) * tile, tile), tile), :].T
        panel_factor(w, u, 0, half, 64, 8)
        for copy in fetch([(u.at[pl.ds(0, half), :], top), (w.at[pl.ds(half, half), :], rest)], sems):
            copy.wait()


def panel_tail(tile, panel, top, rest, before, column, lower, w, u, low, mine, sems):
    core = lax.axis_index("slab") % 2
    half = tile // 2
    holds, pos = holds_panel(panel)

    @pl.when(holds)
    def _():
        for copy in fetch([(top, u.at[pl.ds(0, half), :]), (rest, w.at[pl.ds(half, half), :])], sems):
            copy.wait()
        panel_factor(w, u, half, tile, 64, 8)
        low[...] = u[:, tile:].astype(low.dtype)
        out = pltpu.make_async_copy(low, lower, sems.at[0])
        out.start()
        rows = pl.ds(pl.multiple_of(core * half, half), half)
        mine[pl.ds(pl.multiple_of(pos * tile, tile), tile), :] = u[rows, :tile].T
        mine[pl.ds(pl.multiple_of((1 - pos) * tile, tile), tile), :] = u[rows, tile:].T
        back = pltpu.make_async_copy(mine, column, sems.at[1])
        back.start()
        out.wait()
        back.wait()


def final_kernel(tile, column, own2, own1, ahead2, ahead1, beside, out):
    group = lax.axis_index("blk")
    rows = column.shape[0]
    out[0] = column[...]
    out[2] = own2[...] + ahead2[...].astype(jnp.float32)
    late = jnp.where(group % 2 == 1, own1[...], ahead1[...].astype(jnp.float32))
    out[1] = late + beside[...].astype(jnp.float32)


def reduce_kernel(tile, panel, lower_any, band, out, lower, corner, sems):
    slab = lax.axis_index("slab")
    core = slab % 2
    y_lo = slab // 2
    half = tile // 2
    block = panel[0]

    @pl.when((block // 2 == lax.axis_index("blk")) & (block % 2 != y_lo))
    def _():
        here = out.at[0, pl.ds(pl.multiple_of(y_lo * tile, tile), tile), :]
        for copy in fetch([(lower_any, lower), (here, corner)], sems):
            copy.wait()
        left = lower[...].astype(jnp.float32)
        right = jnp.where(core == 0, left[:, :half], left[:, half:])
        corner[...] = corner[...] - lax.dot_general(
            left, right, (((0,), (0,)), ((), ())), precision=HIGH, preferred_element_type=jnp.float32)
        back = pltpu.make_async_copy(corner, here, sems.at[2])
        back.start()
        back.wait()


def make_body(groups, slabs):
    devices = [(g, s) for g in range(groups) for s in range(slabs)]
    at = lambda g, s: (g % groups) * slabs + s
    forward = lambda s: s % 2 == 0
    hubs = [(g, s) for g, s in devices if (g + s) % 2 == 1]
    far_pairs = [(at(g, s), at(g + (2 if forward(s) else -2), s)) for g, s in devices]
    near_pairs = [(at(g + (-1 if forward(s) else 1), s), at(g, s)) for g, s in hubs]
    slab_pairs = lambda k, among=devices: [(at(g, s), at(g, s ^ k)) for g, s in among]
    ahead_pairs = [(at(g, s), at(g + 2, s)) for g, s in devices]
    even_ahead_pairs = [(at(g, s), at(g + 2, s)) for g, s in devices if g % 2 == 0]
    beside_pairs = [(at(g, s), at(g ^ 1, s)) for g, s in devices]

    hold = lax.optimization_barrier

    def move(value, pairs):
        return lax.ppermute(value, AXES, pairs)

    def body(a_tiles, tile_cols, tile_counts, scaling, panel):
        rows = a_tiles.shape[0]
        blocks = tile_cols.shape[0]
        slots = tile_cols.shape[2]
        tile = rows // blocks
        col_tiles = scaling.shape[0] // tile
        half = tile // 2
        f32 = jnp.float32
        bf16 = jnp.bfloat16
        shape = jax.ShapeDtypeStruct
        scales = scaling.reshape(col_tiles, tile)
        cols = pltpu.SMEM((2, slots), jnp.int32)
        tail = pltpu.VMEM((16, 128), bf16)
        counts = tile_counts[:, 0]
        moved = pltpu.SMEM((8, 128), jnp.int32)
        dma = lambda n: pltpu.SemaphoreType.DMA((n,))
        packed = pl.pallas_call(
            lambda *refs: pack_kernel(slots, col_tiles, *refs),
            out_shape=shape((rows + 16, a_tiles.shape[1]), bf16),
            in_specs=[SMEM, SMEM, ANY], out_specs=ANY, scratch_shapes=[pltpu.VMEM(a_tiles.shape, bf16), cols, tail, dma(9)], name="pack",
        )(tile_cols, counts, a_tiles)
        table = pltpu.SMEM((2, col_tiles + 1), jnp.int32)
        scaled = pltpu.VMEM((tile, tile), bf16)
        sizes = (tile, slots, col_tiles)
        own_tiles, packed = hold((a_tiles, packed))
        x = move(packed, far_pairs)
        y = move(packed, near_pairs)
        give, keep = pl.pallas_call(
            lambda *refs: own_kernel(*sizes, *refs),
            out_shape=(shape((rows + tile, tile), f32), shape((rows + tile, tile), f32)),
            in_specs=[SMEM, SMEM, VMEM, VMEM], out_specs=(VMEM, VMEM),
            scratch_shapes=[cols, table, scaled, pltpu.VMEM((2, rows, tile), f32)], name="plane_zero",
            compiler_params=pltpu.CompilerParams(vmem_limit_bytes=64 * 2**20 - 2**16),
        )(tile_cols, counts, scales, own_tiles)
        got = move(give, slab_pairs(1))
        mine = move(keep[rows:] + got[rows:], slab_pairs(2))
        part = shape((rows, half), bf16)
        two = shape((2 * rows, half), bf16)
        whole = pltpu.VMEM(a_tiles.shape, bf16)
        acc = pltpu.VMEM((4, rows, half), f32)
        p1, p2, p3, kept2 = pl.pallas_call(
            lambda *refs: second_kernel(*sizes, *refs),
            out_shape=(part, part, part, shape((rows, half), f32)),
            in_specs=[SMEM, SMEM, VMEM, ANY, ANY], out_specs=(VMEM,) * 4,
            scratch_shapes=[whole, whole, cols, moved, pltpu.VMEM((1, 16, 128), bf16), pltpu.VMEM((1, 8, 128), jnp.int32), table, scaled, acc, dma(4)],
            name="plane_two",
        )(tile_cols, counts, scales, a_tiles, x)
        y, kept2 = hold((y, kept2))
        q1, q2, q3, kept1 = pl.pallas_call(
            lambda *refs: first_kernel(*sizes, *refs),
            out_shape=(two, two, two, shape((2 * rows, half), f32)),
            in_specs=[SMEM, SMEM, VMEM, ANY, ANY, ANY], out_specs=(VMEM,) * 4,
            scratch_shapes=[whole, whole, whole, cols, moved, moved, pltpu.VMEM((2, 16, 128), bf16), pltpu.VMEM((2, 8, 128), jnp.int32), table, scaled, acc, dma(7)],
            name="plane_one",
        )(tile_cols, counts, scales, a_tiles, x, y)
        r1, r2, r3 = [move(p, slab_pairs(k)) for k, p in ((1, p1), (2, p2), (3, p3))]
        t1, t2, t3 = [move(q, slab_pairs(k, hubs)) for k, q in ((1, q1), (2, q2), (3, q3))]
        core = lax.axis_index("slab") % 2
        wide = lambda value: value.astype(f32)
        r1, r2, r3, mine = hold((r1, r2, r3, mine))
        theirs = move(mine, slab_pairs(1))
        same = kept2 + wide(r2)
        swapped = wide(r1) + wide(r3)
        own2 = jnp.where(core == 0, same, swapped)
        ahead2 = jnp.where(core == 0, swapped, same).astype(bf16)
        ahead2 = move(ahead2, ahead_pairs)
        column, top, rest = pl.pallas_call(
            lambda *refs: panel_head(tile, *refs),
            out_shape=(shape((rows, half), f32), shape((half, rows), f32), shape((half, rows), f32)),
            in_specs=[SMEM] + [VMEM] * 4, out_specs=(VMEM, ANY, ANY),
            scratch_shapes=[pltpu.VMEM((rows, tile), f32), pltpu.VMEM((tile, rows), f32), pltpu.VMEM((tile, rows), f32),
                            dma(2)],
            name="panel_head",
        )(panel, keep, got, mine, theirs)
        t1, t2, t3, column = hold((t1, t2, t3, column))
        out1 = sum(wide(value[:rows]) for value in (kept1, t1, t2, t3))
        own1 = sum(wide(value[rows:]) for value in (kept1, t1, t2, t3))
        beside, ahead1, top = hold((out1.astype(bf16), own1.astype(bf16), top))
        beside = move(beside, beside_pairs)
        ahead1 = move(ahead1, even_ahead_pairs)
        column, lower = pl.pallas_call(
            lambda *refs: panel_tail(tile, *refs),
            out_shape=(shape((rows, half), f32), shape((tile, tile), bf16)),
            in_specs=[SMEM, ANY, ANY, ANY], out_specs=(ANY, ANY), input_output_aliases={3: 0},
            scratch_shapes=[pltpu.VMEM((tile, rows), f32), pltpu.VMEM((tile, rows), f32), pltpu.VMEM((tile, tile), bf16),
                            pltpu.VMEM((rows, half), f32), dma(2)],
            name="panel_tail",
            compiler_params=pltpu.CompilerParams(vmem_limit_bytes=64 * 2**20 - 2**16),
        )(panel, top, rest, column)
        lower = move(lower, slab_pairs(2))
        out = pl.pallas_call(
            lambda *refs: final_kernel(tile, *refs),
            out_shape=shape((3, rows, half), f32),
            in_specs=[VMEM] * 6, out_specs=VMEM, name="assemble",
            compiler_params=pltpu.CompilerParams(vmem_limit_bytes=64 * 2**20 - 2**16),
        )(column, own2, own1, ahead2, ahead1, beside)
        out = pl.pallas_call(
            lambda *refs: reduce_kernel(tile, *refs),
            out_shape=shape((3, rows, half), f32),
            in_specs=[SMEM, ANY, ANY], out_specs=ANY, input_output_aliases={2: 0},
            scratch_shapes=[pltpu.VMEM((tile, tile), bf16), pltpu.VMEM((tile, half), f32), dma(3)], name="reduce",
        )(panel, lower, out)
        return out.transpose(1, 0, 2)

    return body


def solution(mesh):
    return jax.shard_map(
        make_body(mesh.shape["blk"], mesh.shape["slab"]),
        mesh=mesh,
        in_specs=(P("blk", "slab"), P("blk", "slab", None), P("blk", "slab"), P("slab"), P()),
        out_specs=P("blk", None, "slab"),
        check_vma=False,
    )
```

profile of v0, /device:TPU:54, one launch (start us, length us, event | category | flops | bytes accessed | tf_op | source)
XLA Modules:
  0.0 82.7 jit_solution(3785661012759079948)
XLA Ops:
  0.0 3.3 %pack.1 = bf16[528,2048]{1,0:T(8,128)(2,1)} custom-call(s32[2,1,8]{2,1,0:T(1,128)} %refs_0_.10, s32[2]{0:T(128)} %bitcast.2, bf16[512,2048]{1,0:T(8,128)(2,1)} %refs_3_.4), custom_call_target="tpu_custom_call" | custom-call | tf_op jit(solution)/shard_map/pack/pallas_call | solution.py:436
  3.3 1.9 %collective-permute-start = (bf16[528,2048]{1,0:T(8,128)(2,1)}, bf16[528,2048]{1,0:T(8,128)(2,1)}, u32[]{:S(2)}, u32[]{:S(2)}) collective-permute-start(bf16[528,2048]{1,0:T(8,128)(2,1)} %pack.1), channel_id=1, source_target_pairs={{0,8},{1,249},{2,10},{3,251},{4,12},{5,253},{6,14},{7,255},{8,16},... | collective-permute-start | bytes 6488072 | tf_op jit(solution)/shard_map/ppermute | solution.py:418
  5.2 1.3 %collective-permute-start.1 = (bf16[528,2048]{1,0:T(8,128)(2,1)}, bf16[528,2048]{1,0:T(8,128)(2,1)}, u32[]{:S(2)}, u32[]{:S(2)}) collective-permute-start(bf16[528,2048]{1,0:T(8,128)(2,1)} %pack.1), channel_id=1, source_target_pairs={{5,1},{7,3},{0,4},{2,6},{13,9},{15,11},{8,12},{10,14},{21,17},{23,... | collective-permute-start | bytes 6488072 | tf_op jit(solution)/shard_map/ppermute | solution.py:418
  7.1 4.1 %plane_zero.1 = (f32[768,256]{1,0:T(8,128)}, f32[768,256]{1,0:T(8,128)}) custom-call(s32[2,1,8]{2,1,0:T(1,128)} %refs_0_.10, s32[2]{0:T(128)} %bitcast.3, f32[16,256]{1,0:T(8,128)} %reshape.3.refs_2_, bf16[512,2048]{1,0:T(8,128)(2,1)} %refs_3_.4), custom_call_target="tpu_custom_call" | custom-call | tf_op jit(solution)/shard_map/plane_zero/pallas_call | solution.py:447
  11.3 0.8 collective-permute-start.5
  12.1 2.1 %collective-permute-done.5.refs_2_ = f32[768,256]{1,0:T(8,128)S(1)} collective-permute-done((f32[768,256]{1,0:T(8,128)}, f32[768,256]{1,0:T(8,128)S(1)}, u32[]{:S(2)}, u32[]{:S(2)}) %collective-permute-start.5) | collective-permute-done | bytes 786464 | tf_op jit(solution)/shard_map/ppermute | solution.py:418
  14.2 1.1 %slice_add_fusion = f32[256,256]{1,0:T(8,128)S(1)} fusion(f32[768,256]{1,0:T(8,128)S(1)} %collective-permute-done.5.refs_2_, f32[768,256]{1,0:T(8,128)} %get-tuple-element.43.refs_1_), kind=kLoop, calls=%fused_computation | loop fusion | flops 65536 | bytes 786432 | tf_op jit(solution)/shard_map/add | solution.py:455
  15.4 3.2 %collective-permute-start.9 = (f32[256,256]{1,0:T(8,128)S(1)}, f32[256,256]{1,0:T(8,128)S(1)}, u32[]{:S(2)}, u32[]{:S(2)}) collective-permute-start(f32[256,256]{1,0:T(8,128)S(1)} %slice_add_fusion), channel_id=1, source_target_pairs={{0,2},{1,3},{2,0},{3,1},{4,6},{5,7},{6,4},{7,5},{8,10},{9,11},{10,... | collective-permute-start | bytes 786440 | tf_op jit(solution)/shard_map/ppermute | solution.py:418
  18.6 11.9 %collective-permute-done.refs_4_ = bf16[528,2048]{1,0:T(8,128)(2,1)} collective-permute-done((bf16[528,2048]{1,0:T(8,128)(2,1)}, bf16[528,2048]{1,0:T(8,128)(2,1)}, u32[]{:S(2)}, u32[]{:S(2)}) %collective-permute-start) | collective-permute-done | bytes 2162720 | tf_op jit(solution)/shard_map/ppermute | solution.py:418
  30.5 4.6 %plane_two.1 = (bf16[512,128]{1,0:T(8,128)(2,1)}, bf16[512,128]{1,0:T(8,128)(2,1)}, bf16[512,128]{1,0:T(8,128)(2,1)}, f32[512,128]{1,0:T(8,128)}) custom-call(s32[2,1,8]{2,1,0:T(1,128)} %refs_0_.10, s32[2]{0:T(128)} %bitcast.4, f32[16,256]{1,0:T(8,128)} %reshape.3.refs_2_, bf16[512,2048]{1,0:T(8,128)(2,1)} %refs_3_.4, ...), custom_call_target="tpu_custom_call" | custom-call | tf_op jit(solution)/shard_map/plane_two/pallas_call | solution.py:460
  35.7 1.4 %collective-permute-start.7 = (bf16[512,128]{1,0:T(8,128)(2,1)}, bf16[512,128]{1,0:T(8,128)(2,1)S(1)}, u32[]{:S(2)}, u32[]{:S(2)}) collective-permute-start(bf16[512,128]{1,0:T(8,128)(2,1)} %get-tuple-element.46), channel_id=1, source_target_pairs={{0,2},{1,3},{2,0},{3,1},{4,6},{5,7},{6,4},{7,5},{8,10},{9,11},{10,... | collective-permute-start | bytes 393224 | tf_op jit(solution)/shard_map/ppermute | solution.py:418
  37.1 1.4 %collective-permute-done.1.refs_5_ = bf16[528,2048]{1,0:T(8,128)(2,1)} collective-permute-done((bf16[528,2048]{1,0:T(8,128)(2,1)}, bf16[528,2048]{1,0:T(8,128)(2,1)}, u32[]{:S(2)}, u32[]{:S(2)}) %collective-permute-start.1) | collective-permute-done | bytes 2162720 | tf_op jit(solution)/shard_map/ppermute | solution.py:418
  38.5 6.6 %plane_one.1 = (bf16[1024,128]{1,0:T(8,128)(2,1)}, bf16[1024,128]{1,0:T(8,128)(2,1)}, bf16[1024,128]{1,0:T(8,128)(2,1)}, f32[1024,128]{1,0:T(8,128)}) custom-call(s32[2,1,8]{2,1,0:T(1,128)} %refs_0_.10, s32[2]{0:T(128)} %bitcast.5, f32[16,256]{1,0:T(8,128)} %reshape.3.refs_2_, bf16[512,2048]{1,0:T(8,128)(2,1)} %refs_3_.4, ...), custom_call_target="tpu_custom_call" | custom-call | tf_op jit(solution)/shard_map/plane_one/pallas_call | solution.py:468
  45.1 1.4 %collective-permute-start.2 = (bf16[1024,128]{1,0:T(8,128)(2,1)}, bf16[1024,128]{1,0:T(8,128)(2,1)S(1)}, u32[]{:S(2)}, u32[]{:S(2)}) collective-permute-start(bf16[1024,128]{1,0:T(8,128)(2,1)} %get-tuple-element.39), channel_id=1, source_target_pairs={{1,0},{3,2},{4,5},{6,7},{9,8},{11,10},{12,13},{14,15},{17,16},{19,... | collective-permute-start | bytes 786440 | tf_op jit(solution)/shard_map/ppermute | solution.py:418
  46.7 2.2 %collective-permute-start.3 = (bf16[1024,128]{1,0:T(8,128)(2,1)}, bf16[1024,128]{1,0:T(8,128)(2,1)S(1)}, u32[]{:S(2)}, u32[]{:S(2)}) collective-permute-start(bf16[1024,128]{1,0:T(8,128)(2,1)} %get-tuple-element.40), channel_id=1, source_target_pairs={{1,3},{3,1},{4,6},{6,4},{9,11},{11,9},{12,14},{14,12},{17,19},{19,... | collective-permute-start | bytes 786440 | tf_op jit(solution)/shard_map/ppermute | solution.py:418
  48.9 1.3 %collective-permute-start.4 = (bf16[1024,128]{1,0:T(8,128)(2,1)}, bf16[1024,128]{1,0:T(8,128)(2,1)S(1)}, u32[]{:S(2)}, u32[]{:S(2)}) collective-permute-start(bf16[1024,128]{1,0:T(8,128)(2,1)} %get-tuple-element.41), channel_id=1, source_target_pairs={{1,2},{3,0},{4,7},{6,5},{9,10},{11,8},{12,15},{14,13},{17,18},{19,... | collective-permute-start | bytes 786440 | tf_op jit(solution)/shard_map/ppermute | solution.py:418
  51.7 7.5 %collective-permute-start.12 = (bf16[512,128]{1,0:T(8,128)(2,1)}, bf16[512,128]{1,0:T(8,128)(2,1)}, u32[]{:S(2)}, u32[]{:S(2)}) collective-permute-start(bf16[512,128]{1,0:T(8,128)(2,1)} %get-tuple-element.68), channel_id=1, source_target_pairs={{0,8},{1,9},{2,10},{3,11},{4,12},{5,13},{6,14},{7,15},{8,16},{9,17... | collective-permute-start | bytes 393224 | tf_op jit(solution)/shard_map/ppermute | solution.py:418
  60.0 2.4 %panel_head.1 = (f32[512,128]{1,0:T(8,128)}, f32[128,512]{1,0:T(8,128)}, f32[128,512]{1,0:T(8,128)}) custom-call(s32[1]{0:T(128)S(6)} %copy.10.refs_0_, f32[768,256]{1,0:T(8,128)} %get-tuple-element.43.refs_1_, f32[768,256]{1,0:T(8,128)} %copy-done, f32[256,256]{1,0:T(8,128)} %copy-done.2, f32[256,256]{1,0:T(8,128)} %copy-done.3), custom_call_target="tpu_custom_call" | custom-call | tf_op jit(solution)/shard_map/panel_head/pallas_call | solution.py:486
  62.4 0.8 %fusion.1 = (bf16[512,128]{1,0:T(8,128)(2,1)}, f32[512,128]{1,0:T(8,128)}, bf16[512,128]{1,0:T(8,128)(2,1)}) fusion(bf16[1024,128]{1,0:T(8,128)(2,1)S(1)} %collective-permute-done.4, bf16[1024,128]{1,0:T(8,128)(2,1)S(1)} %collective-permute-done.3, bf16[1024,128]{1,0:T(8,128)(2,1)S(1)} %collective-permute-done.2, f32[1024,128]{1,0:T(8,128)S(1)} %copy-done.1), kind=kLoop, calls=%fused_computation.7 | loop fusion | flops 917504 | bytes 1835008 | tf_op jit(solution)/shard_map/convert_element_type | solution.py:497
  63.2 1.3 %collective-permute-start.13 = (bf16[512,128]{1,0:T(8,128)(2,1)}, bf16[512,128]{1,0:T(8,128)(2,1)}, u32[]{:S(2)}, u32[]{:S(2)}) collective-permute-start(bf16[512,128]{1,0:T(8,128)(2,1)} %get-tuple-element.63), channel_id=1, source_target_pairs={{0,8},{1,9},{2,10},{3,11},{8,16},{9,17},{10,18},{11,19},{16,24},{1... | collective-permute-start | bytes 393224 | tf_op jit(solution)/shard_map/ppermute | solution.py:418
  64.5 12.6 %collective-permute-start.11 = (bf16[256,256]{1,0:T(8,128)(2,1)}, bf16[256,256]{1,0:T(8,128)(2,1)}, u32[]{:S(2)}, u32[]{:S(2)}) collective-permute-start(bf16[256,256]{1,0:T(8,128)(2,1)} %get-tuple-element.57), channel_id=1, source_target_pairs={{0,2},{1,3},{2,0},{3,1},{4,6},{5,7},{6,4},{7,5},{8,10},{9,11},{10,... | collective-permute-start | bytes 393224 | tf_op jit(solution)/shard_map/ppermute | solution.py:418
  77.2 2.2 %assemble.1.refs_2_ = f32[3,512,128]{2,1,0:T(8,128)} custom-call(f32[512,128]{1,0:T(8,128)} %get-tuple-element.58.refs_0_, f32[512,128]{1,0:T(8,128)} %get-tuple-element.69.refs_1_, f32[512,128]{1,0:T(8,128)} %get-tuple-element.66.refs_2_, bf16[512,128]{1,0:T(8,128)(2,1)} %collective-permute-done.12.refs_3_, ...), custom_call_target="tpu_custom_call" | custom-call | tf_op jit(solution)/shard_map/assemble/pallas_call | solution.py:510
  79.4 1.1 %collective-permute-done.11.refs_1_ = bf16[256,256]{1,0:T(8,128)(2,1)} collective-permute-done((bf16[256,256]{1,0:T(8,128)(2,1)}, bf16[256,256]{1,0:T(8,128)(2,1)}, u32[]{:S(2)}, u32[]{:S(2)}) %collective-permute-start.11) | collective-permute-done | bytes 131104 | tf_op jit(solution)/shard_map/ppermute | solution.py:418
  80.4 2.1 %reduce.1 = f32[3,512,128]{2,1,0:T(8,128)} custom-call(s32[1]{0:T(128)S(6)} %copy.10.refs_0_, bf16[256,256]{1,0:T(8,128)(2,1)} %collective-permute-done.11.refs_1_, f32[3,512,128]{2,1,0:T(8,128)} %assemble.1.refs_2_), custom_call_target="tpu_custom_call", output_to_operand_aliasing={{}: (2, {})} | custom-call | tf_op jit(solution)/shard_map/reduce/pallas_call | solution.py:516
  (30 shorter events, 2.9 us)
Async XLA Ops:
  0.0 6.5 %copy-start.5 = (f32[4096]{0:T(1024)S(1)}, f32[4096]{0:T(1024)}, u32[]{:S(2)}) copy-start(f32[4096]{0:T(1024)} %param.8) | copy-start | bytes 49156
  3.3 27.1 %collective-permute-start = (bf16[528,2048]{1,0:T(8,128)(2,1)}, bf16[528,2048]{1,0:T(8,128)(2,1)}, u32[]{:S(2)}, u32[]{:S(2)}) collective-permute-start(bf16[528,2048]{1,0:T(8,128)(2,1)} %pack.1), channel_id=1, source_target_pairs={{0,8},{1,249},{2,10},{3,251},{4,12},{5,253},{6,14},{7,255},{8,16},... | collective-permute-start | bytes 6488072 | tf_op jit(solution)/shard_map/ppermute | solution.py:418
  5.2 33.2 %collective-permute-start.1 = (bf16[528,2048]{1,0:T(8,128)(2,1)}, bf16[528,2048]{1,0:T(8,128)(2,1)}, u32[]{:S(2)}, u32[]{:S(2)}) collective-permute-start(bf16[528,2048]{1,0:T(8,128)(2,1)} %pack.1), channel_id=1, source_target_pairs={{5,1},{7,3},{0,4},{2,6},{13,9},{15,11},{8,12},{10,14},{21,17},{23,... | collective-permute-start | bytes 6488072 | tf_op jit(solution)/shard_map/ppermute | solution.py:418
  11.3 2.9 %collective-permute-start.5 = (f32[768,256]{1,0:T(8,128)}, f32[768,256]{1,0:T(8,128)S(1)}, u32[]{:S(2)}, u32[]{:S(2)}) collective-permute-start(f32[768,256]{1,0:T(8,128)} %get-tuple-element.44), channel_id=1, source_target_pairs={{0,1},{1,0},{2,3},{3,2},{4,5},{5,4},{6,7},{7,6},{8,9},{9,8},{10,11... | collective-permute-start | bytes 2359304 | tf_op jit(solution)/shard_map/ppermute | solution.py:418
  14.2 20.9 %copy-start = (f32[768,256]{1,0:T(8,128)}, f32[768,256]{1,0:T(8,128)S(1)}, u32[]{:S(2)}) copy-start(f32[768,256]{1,0:T(8,128)S(1)} %collective-permute-done.5.refs_2_) | copy-start | bytes 2359300
  15.4 31.2 %collective-permute-start.9 = (f32[256,256]{1,0:T(8,128)S(1)}, f32[256,256]{1,0:T(8,128)S(1)}, u32[]{:S(2)}, u32[]{:S(2)}) collective-permute-start(f32[256,256]{1,0:T(8,128)S(1)} %slice_add_fusion), channel_id=1, source_target_pairs={{0,2},{1,3},{2,0},{3,1},{4,6},{5,7},{6,4},{7,5},{8,10},{9,11},{10,... | collective-permute-start | bytes 786440 | tf_op jit(solution)/shard_map/ppermute | solution.py:418
  35.1 11.5 %collective-permute-start.6 = (bf16[512,128]{1,0:T(8,128)(2,1)}, bf16[512,128]{1,0:T(8,128)(2,1)S(1)}, u32[]{:S(2)}, u32[]{:S(2)}) collective-permute-start(bf16[512,128]{1,0:T(8,128)(2,1)} %get-tuple-element.45), channel_id=1, source_target_pairs={{0,1},{1,0},{2,3},{3,2},{4,5},{5,4},{6,7},{7,6},{8,9},{9,8},{10,11... | collective-permute-start | bytes 393224 | tf_op jit(solution)/shard_map/ppermute | solution.py:418
  35.7 10.9 %collective-permute-start.7 = (bf16[512,128]{1,0:T(8,128)(2,1)}, bf16[512,128]{1,0:T(8,128)(2,1)S(1)}, u32[]{:S(2)}, u32[]{:S(2)}) collective-permute-start(bf16[512,128]{1,0:T(8,128)(2,1)} %get-tuple-element.46), channel_id=1, source_target_pairs={{0,2},{1,3},{2,0},{3,1},{4,6},{5,7},{6,4},{7,5},{8,10},{9,11},{10,... | collective-permute-start | bytes 393224 | tf_op jit(solution)/shard_map/ppermute | solution.py:418
  37.0 9.6 %collective-permute-start.8 = (bf16[512,128]{1,0:T(8,128)(2,1)}, bf16[512,128]{1,0:T(8,128)(2,1)S(1)}, u32[]{:S(2)}, u32[]{:S(2)}) collective-permute-start(bf16[512,128]{1,0:T(8,128)(2,1)} %get-tuple-element.47), channel_id=1, source_target_pairs={{0,3},{1,2},{2,1},{3,0},{4,7},{5,6},{6,5},{7,4},{8,11},{9,10},{10,... | collective-permute-start | bytes 393224 | tf_op jit(solution)/shard_map/ppermute | solution.py:418
  38.5 12.4 %copy-start.4 = (f32[512,128]{1,0:T(8,128)S(1)}, f32[512,128]{1,0:T(8,128)}, u32[]{:S(2)}) copy-start(f32[512,128]{1,0:T(8,128)} %get-tuple-element.59) | copy-start | bytes 786436
  45.1 17.3 %copy-start.1 = (f32[1024,128]{1,0:T(8,128)S(1)}, f32[1024,128]{1,0:T(8,128)}, u32[]{:S(2)}) copy-start(f32[1024,128]{1,0:T(8,128)} %get-tuple-element.38) | copy-start | bytes 1572868
  45.1 17.2 %collective-permute-start.2 = (bf16[1024,128]{1,0:T(8,128)(2,1)}, bf16[1024,128]{1,0:T(8,128)(2,1)S(1)}, u32[]{:S(2)}, u32[]{:S(2)}) collective-permute-start(bf16[1024,128]{1,0:T(8,128)(2,1)} %get-tuple-element.39), channel_id=1, source_target_pairs={{1,0},{3,2},{4,5},{6,7},{9,8},{11,10},{12,13},{14,15},{17,16},{19,... | collective-permute-start | bytes 786440 | tf_op jit(solution)/shard_map/ppermute | solution.py:418
  46.6 12.7 %copy-start.2 = (f32[256,256]{1,0:T(8,128)}, f32[256,256]{1,0:T(8,128)S(1)}, u32[]{:S(2)}) copy-start(f32[256,256]{1,0:T(8,128)S(1)} %collective-permute-done.9.refs_3_) | copy-start | bytes 786436
  46.6 12.6 %collective-permute-start.10 = (f32[256,256]{1,0:T(8,128)S(1)}, f32[256,256]{1,0:T(8,128)S(1)}, u32[]{:S(2)}, u32[]{:S(2)}) collective-permute-start(f32[256,256]{1,0:T(8,128)S(1)} %collective-permute-done.9.refs_3_), channel_id=1, source_target_pairs={{0,1},{1,0},{2,3},{3,2},{4,5},{5,4},{6,7},{7,6},{8,9},{9,8},{10,11... | collective-permute-start | bytes 786440 | tf_op jit(solution)/shard_map/ppermute | solution.py:418
  46.7 15.6 %collective-permute-start.3 = (bf16[1024,128]{1,0:T(8,128)(2,1)}, bf16[1024,128]{1,0:T(8,128)(2,1)S(1)}, u32[]{:S(2)}, u32[]{:S(2)}) collective-permute-start(bf16[1024,128]{1,0:T(8,128)(2,1)} %get-tuple-element.40), channel_id=1, source_target_pairs={{1,3},{3,1},{4,6},{6,4},{9,11},{11,9},{12,14},{14,12},{17,19},{19,... | collective-permute-start | bytes 786440 | tf_op jit(solution)/shard_map/ppermute | solution.py:418
  48.9 13.4 %collective-permute-start.4 = (bf16[1024,128]{1,0:T(8,128)(2,1)}, bf16[1024,128]{1,0:T(8,128)(2,1)S(1)}, u32[]{:S(2)}, u32[]{:S(2)}) collective-permute-start(bf16[1024,128]{1,0:T(8,128)(2,1)} %get-tuple-element.41), channel_id=1, source_target_pairs={{1,2},{3,0},{4,7},{6,5},{9,10},{11,8},{12,15},{14,13},{17,18},{19,... | collective-permute-start | bytes 786440 | tf_op jit(solution)/shard_map/ppermute | solution.py:418
  51.7 25.4 %collective-permute-start.12 = (bf16[512,128]{1,0:T(8,128)(2,1)}, bf16[512,128]{1,0:T(8,128)(2,1)}, u32[]{:S(2)}, u32[]{:S(2)}) collective-permute-start(bf16[512,128]{1,0:T(8,128)(2,1)} %get-tuple-element.68), channel_id=1, source_target_pairs={{0,8},{1,9},{2,10},{3,11},{4,12},{5,13},{6,14},{7,15},{8,16},{9,17... | collective-permute-start | bytes 393224 | tf_op jit(solution)/shard_map/ppermute | solution.py:418
  59.3 0.7 copy-start.3
  63.2 14.0 %collective-permute-start.13 = (bf16[512,128]{1,0:T(8,128)(2,1)}, bf16[512,128]{1,0:T(8,128)(2,1)}, u32[]{:S(2)}, u32[]{:S(2)}) collective-permute-start(bf16[512,128]{1,0:T(8,128)(2,1)} %get-tuple-element.63), channel_id=1, source_target_pairs={{0,8},{1,9},{2,10},{3,11},{8,16},{9,17},{10,18},{11,19},{16,24},{1... | collective-permute-start | bytes 393224 | tf_op jit(solution)/shard_map/ppermute | solution.py:418
  64.5 12.7 %collective-permute-start.14 = (bf16[512,128]{1,0:T(8,128)(2,1)}, bf16[512,128]{1,0:T(8,128)(2,1)}, u32[]{:S(2)}, u32[]{:S(2)}) collective-permute-start(bf16[512,128]{1,0:T(8,128)(2,1)} %get-tuple-element.64), channel_id=1, source_target_pairs={{0,4},{1,5},{2,6},{3,7},{4,0},{5,1},{6,2},{7,3},{8,12},{9,13},{10,... | collective-permute-start | bytes 393224 | tf_op jit(solution)/shard_map/ppermute | solution.py:418
  64.5 15.9 %collective-permute-start.11 = (bf16[256,256]{1,0:T(8,128)(2,1)}, bf16[256,256]{1,0:T(8,128)(2,1)}, u32[]{:S(2)}, u32[]{:S(2)}) collective-permute-start(bf16[256,256]{1,0:T(8,128)(2,1)} %get-tuple-element.57), channel_id=1, source_target_pairs={{0,2},{1,3},{2,0},{3,1},{4,6},{5,7},{6,4},{7,5},{8,10},{9,11},{10,... | collective-permute-start | bytes 393224 | tf_op jit(solution)/shard_map/ppermute | solution.py:418
where the time goes:
time: 81.3 us; the launch traced here: 82.7 us
  starting transfers between devices  35.8 us (44%)
  Pallas kernels  25.3 us (31%)
  waiting for transfers between devices  16.4 us (20%)
  other arithmetic  2.81 us (3%)
  local copies, waits for them, and re-layouts  1.32 us (2%)
  between operations  1.02 us (1%)
    ppermute x15, starting transfers between devices, move(): return lax.ppermute(value, AXES, pairs)  35.8 us
    ppermute x15, waiting for transfers between devices, move(): return lax.ppermute(value, AXES, pairs)  16.4 us
    pallas_call x1, Pallas kernels, body(): pl.pallas_call(lambda *refs: first_kernel(*sizes, *refs), out_shape=(two,...  6.61 us
    pallas_call x1, Pallas kernels, body(): pl.pallas_call(lambda *refs: second_kernel(*sizes, *refs), out_shape=(par...  4.6 us
    pallas_call x1, Pallas kernels, body(): pl.pallas_call(lambda *refs: own_kernel(*sizes, *refs), out_shape=(shape(...  4.13 us
    pallas_call x1, Pallas kernels, body(): pl.pallas_call(lambda *refs: pack_kernel(slots, col_tiles, *refs), out_sh...  3.32 us
    pallas_call x1, Pallas kernels, body(): pl.pallas_call(lambda *refs: panel_head(tile, *refs), out_shape=(shape((r...  2.37 us
    pallas_call x1, Pallas kernels, body(): pl.pallas_call(lambda *refs: final_kernel(tile, *refs), out_shape=shape((...  2.2 us
  transfers between devices with their start and end apart: 15, of which 4 were waited for; matrix products, arithmetic and copies ran while one was open for 4% of the time, Pallas kernels for 24%

commit v1 on v0

--- a/solution.py
+++ b/solution.py
@@ -482,7 +482,6 @@
         swapped = wide(r1) + wide(r3)
         own2 = jnp.where(core == 0, same, swapped)
         ahead2 = jnp.where(core == 0, swapped, same).astype(bf16)
-        ahead2 = move(ahead2, ahead_pairs)
         column, top, rest = pl.pallas_call(
             lambda *refs: panel_head(tile, *refs),
             out_shape=(shape((rows, half), f32), shape((half, rows), f32), shape((half, rows), f32)),
@@ -491,7 +490,8 @@
                             dma(2)],
             name="panel_head",
         )(panel, keep, got, mine, theirs)
-        t1, t2, t3, column = hold((t1, t2, t3, column))
+        t1, t2, t3, column, ahead2 = hold((t1, t2, t3, column, ahead2))
+        ahead2 = move(ahead2, ahead_pairs)
         out1 = sum(wide(value[:rows]) for value in (kept1, t1, t2, t3))
         own1 = sum(wide(value[rows:]) for value in (kept1, t1, t2, t3))
         beside, ahead1, top = hold((out1.astype(bf16), own1.astype(bf16), top))

time: 81.3 us -> 78.9 us (0.970)
  the two profiles are of different devices: /device:TPU:54 before, /device:TPU:100 now
where the time goes in v1:
time: 78.9 us; the launch traced here: 78.1 us
  starting transfers between devices  26.8 us (34%)
  waiting for transfers between devices  25.9 us (33%)
  Pallas kernels  20.4 us (26%)
  other arithmetic  2.81 us (4%)
  local copies, waits for them, and re-layouts  1.32 us (2%)
  between operations  0.96 us (1%)
    ppermute x15, starting transfers between devices, move(): return lax.ppermute(value, AXES, pairs)  26.8 us
    ppermute x15, waiting for transfers between devices, move(): return lax.ppermute(value, AXES, pairs)  25.9 us
    pallas_call x1, Pallas kernels, body(): pl.pallas_call(lambda *refs: own_kernel(*sizes, *refs), out_shape=(shape(...  5.34 us
    pallas_call x1, Pallas kernels, body(): pl.pallas_call(lambda *refs: second_kernel(*sizes, *refs), out_shape=(par...  5.02 us
    pallas_call x1, Pallas kernels, body(): pl.pallas_call(lambda *refs: pack_kernel(slots, col_tiles, *refs), out_sh...  3.32 us
    pallas_call x1, Pallas kernels, body(): pl.pallas_call(lambda *refs: panel_head(tile, *refs), out_shape=(shape((r...  2.37 us
    pallas_call x1, Pallas kernels, body(): pl.pallas_call(lambda *refs: final_kernel(tile, *refs), out_shape=shape((...  2.2 us
    pallas_call x1, Pallas kernels, body(): pl.pallas_call(lambda *refs: first_kernel(*sizes, *refs), out_shape=(two,...  2.04 us
  transfers between devices with their start and end apart: 15, of which 8 were waited for; matrix products, arithmetic and copies ran while one was open for 3% of the time, Pallas kernels for 22%

profile of v1, /device:TPU:100, one launch (start us, length us, event | category | flops | bytes accessed | tf_op | source)
XLA Modules:
  0.0 78.1 jit_solution(17166678855484868470)
XLA Ops:
  0.0 3.3 %pack.1 = bf16[528,2048]{1,0:T(8,128)(2,1)} custom-call(s32[2,1,8]{2,1,0:T(1,128)} %refs_0_.10, s32[2]{0:T(128)} %bitcast.2, bf16[512,2048]{1,0:T(8,128)(2,1)} %refs_3_.4), custom_call_target="tpu_custom_call" | custom-call | tf_op jit(solution)/shard_map/pack/pallas_call | solution.py:436
  3.3 1.3 %collective-permute-start = (bf16[528,2048]{1,0:T(8,128)(2,1)}, bf16[528,2048]{1,0:T(8,128)(2,1)}, u32[]{:S(2)}, u32[]{:S(2)}) collective-permute-start(bf16[528,2048]{1,0:T(8,128)(2,1)} %pack.1), channel_id=1, source_target_pairs={{0,8},{1,249},{2,10},{3,251},{4,12},{5,253},{6,14},{7,255},{8,16},... | collective-permute-start | bytes 6488072 | tf_op jit(solution)/shard_map/ppermute | solution.py:418
  4.6 6.4 %collective-permute-start.1 = (bf16[528,2048]{1,0:T(8,128)(2,1)}, bf16[528,2048]{1,0:T(8,128)(2,1)}, u32[]{:S(2)}, u32[]{:S(2)}) collective-permute-start(bf16[528,2048]{1,0:T(8,128)(2,1)} %pack.1), channel_id=1, source_target_pairs={{5,1},{7,3},{0,4},{2,6},{13,9},{15,11},{8,12},{10,14},{21,17},{23,... | collective-permute-start | bytes 6488072 | tf_op jit(solution)/shard_map/ppermute | solution.py:418
  11.7 5.3 %plane_zero.1 = (f32[768,256]{1,0:T(8,128)}, f32[768,256]{1,0:T(8,128)}) custom-call(s32[2,1,8]{2,1,0:T(1,128)} %refs_0_.10, s32[2]{0:T(128)} %bitcast.3, f32[16,256]{1,0:T(8,128)} %reshape.3.refs_2_, bf16[512,2048]{1,0:T(8,128)(2,1)} %refs_3_.4), custom_call_target="tpu_custom_call" | custom-call | tf_op jit(solution)/shard_map/plane_zero/pallas_call | solution.py:447
  17.0 2.5 %collective-permute-done.5.refs_2_ = f32[768,256]{1,0:T(8,128)S(1)} collective-permute-done((f32[768,256]{1,0:T(8,128)}, f32[768,256]{1,0:T(8,128)S(1)}, u32[]{:S(2)}, u32[]{:S(2)}) %collective-permute-start.5) | collective-permute-done | bytes 786464 | tf_op jit(solution)/shard_map/ppermute | solution.py:418
  19.5 1.1 %slice_add_fusion = f32[256,256]{1,0:T(8,128)S(1)} fusion(f32[768,256]{1,0:T(8,128)S(1)} %collective-permute-done.5.refs_2_, f32[768,256]{1,0:T(8,128)} %get-tuple-element.44.refs_1_), kind=kLoop, calls=%fused_computation | loop fusion | flops 65536 | bytes 786432 | tf_op jit(solution)/shard_map/add | solution.py:455
  20.9 9.6 %collective-permute-done.refs_4_ = bf16[528,2048]{1,0:T(8,128)(2,1)} collective-permute-done((bf16[528,2048]{1,0:T(8,128)(2,1)}, bf16[528,2048]{1,0:T(8,128)(2,1)}, u32[]{:S(2)}, u32[]{:S(2)}) %collective-permute-start) | collective-permute-done | bytes 2162720 | tf_op jit(solution)/shard_map/ppermute | solution.py:418
  30.5 5.0 %plane_two.1 = (bf16[512,128]{1,0:T(8,128)(2,1)}, bf16[512,128]{1,0:T(8,128)(2,1)}, bf16[512,128]{1,0:T(8,128)(2,1)}, f32[512,128]{1,0:T(8,128)}) custom-call(s32[2,1,8]{2,1,0:T(1,128)} %refs_0_.10, s32[2]{0:T(128)} %bitcast.4, f32[16,256]{1,0:T(8,128)} %reshape.3.refs_2_, bf16[512,2048]{1,0:T(8,128)(2,1)} %refs_3_.4, ...), custom_call_target="tpu_custom_call" | custom-call | tf_op jit(solution)/shard_map/plane_two/pallas_call | solution.py:460
  36.1 1.4 %collective-permute-start.8 = (bf16[512,128]{1,0:T(8,128)(2,1)}, bf16[512,128]{1,0:T(8,128)(2,1)S(1)}, u32[]{:S(2)}, u32[]{:S(2)}) collective-permute-start(bf16[512,128]{1,0:T(8,128)(2,1)} %get-tuple-element.48), channel_id=1, source_target_pairs={{0,3},{1,2},{2,1},{3,0},{4,7},{5,6},{6,5},{7,4},{8,11},{9,10},{10,... | collective-permute-start | bytes 393224 | tf_op jit(solution)/shard_map/ppermute | solution.py:418
  37.6 2.0 %plane_one.1 = (bf16[1024,128]{1,0:T(8,128)(2,1)}, bf16[1024,128]{1,0:T(8,128)(2,1)}, bf16[1024,128]{1,0:T(8,128)(2,1)}, f32[1024,128]{1,0:T(8,128)}) custom-call(s32[2,1,8]{2,1,0:T(1,128)} %refs_0_.10, s32[2]{0:T(128)} %bitcast.5, f32[16,256]{1,0:T(8,128)} %reshape.3.refs_2_, bf16[512,2048]{1,0:T(8,128)(2,1)} %refs_3_.4, ...), custom_call_target="tpu_custom_call" | custom-call | tf_op jit(solution)/shard_map/plane_one/pallas_call | solution.py:468
  39.6 1.4 %collective-permute-start.2 = (bf16[1024,128]{1,0:T(8,128)(2,1)}, bf16[1024,128]{1,0:T(8,128)(2,1)S(1)}, u32[]{:S(2)}, u32[]{:S(2)}) collective-permute-start(bf16[1024,128]{1,0:T(8,128)(2,1)} %get-tuple-element.40), channel_id=1, source_target_pairs={{1,0},{3,2},{4,5},{6,7},{9,8},{11,10},{12,13},{14,15},{17,16},{19,... | collective-permute-start | bytes 786440 | tf_op jit(solution)/shard_map/ppermute | solution.py:418
  41.1 1.6 %collective-permute-done.9.refs_3_ = f32[256,256]{1,0:T(8,128)S(1)} collective-permute-done((f32[256,256]{1,0:T(8,128)S(1)}, f32[256,256]{1,0:T(8,128)S(1)}, u32[]{:S(2)}, u32[]{:S(2)}) %collective-permute-start.9) | collective-permute-done | bytes 262176 | tf_op jit(solution)/shard_map/ppermute | solution.py:418
  42.7 2.4 %collective-permute-done.7 = bf16[512,128]{1,0:T(8,128)(2,1)S(1)} collective-permute-done((bf16[512,128]{1,0:T(8,128)(2,1)}, bf16[512,128]{1,0:T(8,128)(2,1)S(1)}, u32[]{:S(2)}, u32[]{:S(2)}) %collective-permute-start.7) | collective-permute-done | bytes 131104 | tf_op jit(solution)/shard_map/ppermute | solution.py:418
  45.5 1.0 %collective-permute-start.10 = (f32[256,256]{1,0:T(8,128)S(1)}, f32[256,256]{1,0:T(8,128)S(1)}, u32[]{:S(2)}, u32[]{:S(2)}) collective-permute-start(f32[256,256]{1,0:T(8,128)S(1)} %collective-permute-done.9.refs_3_), channel_id=1, source_target_pairs={{0,1},{1,0},{2,3},{3,2},{4,5},{5,4},{6,7},{7,6},{8,9},{9,8},{10,11... | collective-permute-start | bytes 786440 | tf_op jit(solution)/shard_map/ppermute | solution.py:418
  47.2 1.3 %collective-permute-start.4 = (bf16[1024,128]{1,0:T(8,128)(2,1)}, bf16[1024,128]{1,0:T(8,128)(2,1)S(1)}, u32[]{:S(2)}, u32[]{:S(2)}) collective-permute-start(bf16[1024,128]{1,0:T(8,128)(2,1)} %get-tuple-element.42), channel_id=1, source_target_pairs={{1,2},{3,0},{4,7},{6,5},{9,10},{11,8},{12,15},{14,13},{17,18},{19,... | collective-permute-start | bytes 786440 | tf_op jit(solution)/shard_map/ppermute | solution.py:418
  49.1 0.8 %fusion = (f32[512,128]{1,0:T(8,128)}, bf16[512,128]{1,0:T(8,128)(2,1)}) fusion(bf16[512,128]{1,0:T(8,128)(2,1)S(1)} %collective-permute-done.8, bf16[512,128]{1,0:T(8,128)(2,1)S(1)} %collective-permute-done.6, f32[512,128]{1,0:T(8,128)S(1)} %copy-done.4, bf16[512,128]{1,0:T(8,128)(2,1)S(1)} %collective-permute-done.7, pred[]{:T(512)S(6)} %eq.6), kind=kLoop, calls=%fused_computation.6 | loop fusion | flops 524288 | bytes 1048577 | tf_op jit(solution)/shard_map/jit(_where)/select_n | solution.py:483
  50.6 2.4 %panel_head.1 = (f32[512,128]{1,0:T(8,128)}, f32[128,512]{1,0:T(8,128)}, f32[128,512]{1,0:T(8,128)}) custom-call(s32[1]{0:T(128)S(6)} %copy.10.refs_0_, f32[768,256]{1,0:T(8,128)} %get-tuple-element.44.refs_1_, f32[768,256]{1,0:T(8,128)} %copy-done, f32[256,256]{1,0:T(8,128)} %copy-done.2, f32[256,256]{1,0:T(8,128)} %copy-done.3), custom_call_target="tpu_custom_call" | custom-call | tf_op jit(solution)/shard_map/panel_head/pallas_call | solution.py:485
  53.0 3.8 %collective-permute-done.4 = bf16[1024,128]{1,0:T(8,128)(2,1)S(1)} collective-permute-done((bf16[1024,128]{1,0:T(8,128)(2,1)}, bf16[1024,128]{1,0:T(8,128)(2,1)S(1)}, u32[]{:S(2)}, u32[]{:S(2)}) %collective-permute-start.4) | collective-permute-done | bytes 262176 | tf_op jit(solution)/shard_map/ppermute | solution.py:418
  56.8 0.8 %fusion.1 = (bf16[512,128]{1,0:T(8,128)(2,1)}, f32[512,128]{1,0:T(8,128)}, bf16[512,128]{1,0:T(8,128)(2,1)}) fusion(bf16[1024,128]{1,0:T(8,128)(2,1)S(1)} %collective-permute-done.4, bf16[1024,128]{1,0:T(8,128)(2,1)S(1)} %collective-permute-done.3, bf16[1024,128]{1,0:T(8,128)(2,1)S(1)} %collective-permute-done.2, f32[1024,128]{1,0:T(8,128)S(1)} %copy-done.1), kind=kLoop, calls=%fused_computation.7 | loop fusion | flops 917504 | bytes 1835008 | tf_op jit(solution)/shard_map/convert_element_type | solution.py:497
  57.7 4.5 %collective-permute-start.12 = (bf16[512,128]{1,0:T(8,128)(2,1)}, bf16[512,128]{1,0:T(8,128)(2,1)}, u32[]{:S(2)}, u32[]{:S(2)}) collective-permute-start(bf16[512,128]{1,0:T(8,128)(2,1)} %get-tuple-element.64), channel_id=1, source_target_pairs={{0,8},{1,9},{2,10},{3,11},{4,12},{5,13},{6,14},{7,15},{8,16},{9,17... | collective-permute-start | bytes 393224 | tf_op jit(solution)/shard_map/ppermute | solution.py:418
  62.1 5.8 %collective-permute-start.13 = (bf16[512,128]{1,0:T(8,128)(2,1)}, bf16[512,128]{1,0:T(8,128)(2,1)}, u32[]{:S(2)}, u32[]{:S(2)}) collective-permute-start(bf16[512,128]{1,0:T(8,128)(2,1)} %get-tuple-element.65), channel_id=1, source_target_pairs={{0,8},{1,9},{2,10},{3,11},{8,16},{9,17},{10,18},{11,19},{16,24},{1... | collective-permute-start | bytes 393224 | tf_op jit(solution)/shard_map/ppermute | solution.py:418
  68.2 1.8 %collective-permute-start.11 = (bf16[256,256]{1,0:T(8,128)(2,1)}, bf16[256,256]{1,0:T(8,128)(2,1)}, u32[]{:S(2)}, u32[]{:S(2)}) collective-permute-start(bf16[256,256]{1,0:T(8,128)(2,1)} %get-tuple-element.62), channel_id=1, source_target_pairs={{0,2},{1,3},{2,0},{3,1},{4,6},{5,7},{6,4},{7,5},{8,10},{9,11},{10,... | collective-permute-start | bytes 393224 | tf_op jit(solution)/shard_map/ppermute | solution.py:418
  70.7 5.0 %collective-permute-done.14.refs_5_ = bf16[512,128]{1,0:T(8,128)(2,1)} collective-permute-done((bf16[512,128]{1,0:T(8,128)(2,1)}, bf16[512,128]{1,0:T(8,128)(2,1)}, u32[]{:S(2)}, u32[]{:S(2)}) %collective-permute-start.14) | collective-permute-done | bytes 131104 | tf_op jit(solution)/shard_map/ppermute | solution.py:418
  75.7 2.2 %assemble.1.refs_2_ = f32[3,512,128]{2,1,0:T(8,128)} custom-call(f32[512,128]{1,0:T(8,128)} %get-tuple-element.63.refs_0_, f32[512,128]{1,0:T(8,128)} %get-tuple-element.70.refs_1_, f32[512,128]{1,0:T(8,128)} %get-tuple-element.68.refs_2_, bf16[512,128]{1,0:T(8,128)(2,1)} %collective-permute-done.12.refs_3_, ...), custom_call_target="tpu_custom_call" | custom-call | tf_op jit(solution)/shard_map/assemble/pallas_call | solution.py:510
  (30 shorter events, 4.3 us)
Async XLA Ops:
  0.0 11.0 %copy-start.5 = (f32[4096]{0:T(1024)S(1)}, f32[4096]{0:T(1024)}, u32[]{:S(2)}) copy-start(f32[4096]{0:T(1024)} %param.8) | copy-start | bytes 49156
  3.3 27.1 %collective-permute-start = (bf16[528,2048]{1,0:T(8,128)(2,1)}, bf16[528,2048]{1,0:T(8,128)(2,1)}, u32[]{:S(2)}, u32[]{:S(2)}) collective-permute-start(bf16[528,2048]{1,0:T(8,128)(2,1)} %pack.1), channel_id=1, source_target_pairs={{0,8},{1,249},{2,10},{3,251},{4,12},{5,253},{6,14},{7,255},{8,16},... | collective-permute-start | bytes 6488072 | tf_op jit(solution)/shard_map/ppermute | solution.py:418
  4.6 33.0 %collective-permute-start.1 = (bf16[528,2048]{1,0:T(8,128)(2,1)}, bf16[528,2048]{1,0:T(8,128)(2,1)}, u32[]{:S(2)}, u32[]{:S(2)}) collective-permute-start(bf16[528,2048]{1,0:T(8,128)(2,1)} %pack.1), channel_id=1, source_target_pairs={{5,1},{7,3},{0,4},{2,6},{13,9},{15,11},{8,12},{10,14},{21,17},{23,... | collective-permute-start | bytes 6488072 | tf_op jit(solution)/shard_map/ppermute | solution.py:418
  17.0 2.5 %collective-permute-start.5 = (f32[768,256]{1,0:T(8,128)}, f32[768,256]{1,0:T(8,128)S(1)}, u32[]{:S(2)}, u32[]{:S(2)}) collective-permute-start(f32[768,256]{1,0:T(8,128)} %get-tuple-element.45), channel_id=1, source_target_pairs={{0,1},{1,0},{2,3},{3,2},{4,5},{5,4},{6,7},{7,6},{8,9},{9,8},{10,11... | collective-permute-start | bytes 2359304 | tf_op jit(solution)/shard_map/ppermute | solution.py:418
  19.5 16.0 %copy-start = (f32[768,256]{1,0:T(8,128)}, f32[768,256]{1,0:T(8,128)S(1)}, u32[]{:S(2)}) copy-start(f32[768,256]{1,0:T(8,128)S(1)} %collective-permute-done.5.refs_2_) | copy-start | bytes 2359300
  20.6 22.0 %collective-permute-start.9 = (f32[256,256]{1,0:T(8,128)S(1)}, f32[256,256]{1,0:T(8,128)S(1)}, u32[]{:S(2)}, u32[]{:S(2)}) collective-permute-start(f32[256,256]{1,0:T(8,128)S(1)} %slice_add_fusion), channel_id=1, source_target_pairs={{0,2},{1,3},{2,0},{3,1},{4,6},{5,7},{6,4},{7,5},{8,10},{9,11},{10,... | collective-permute-start | bytes 786440 | tf_op jit(solution)/shard_map/ppermute | solution.py:418
  35.5 7.2 %collective-permute-start.6 = (bf16[512,128]{1,0:T(8,128)(2,1)}, bf16[512,128]{1,0:T(8,128)(2,1)S(1)}, u32[]{:S(2)}, u32[]{:S(2)}) collective-permute-start(bf16[512,128]{1,0:T(8,128)(2,1)} %get-tuple-element.46), channel_id=1, source_target_pairs={{0,1},{1,0},{2,3},{3,2},{4,5},{5,4},{6,7},{7,6},{8,9},{9,8},{10,11... | collective-permute-start | bytes 393224 | tf_op jit(solution)/shard_map/ppermute | solution.py:418
  36.1 9.0 %collective-permute-start.7 = (bf16[512,128]{1,0:T(8,128)(2,1)}, bf16[512,128]{1,0:T(8,128)(2,1)S(1)}, u32[]{:S(2)}, u32[]{:S(2)}) collective-permute-start(bf16[512,128]{1,0:T(8,128)(2,1)} %get-tuple-element.47), channel_id=1, source_target_pairs={{0,2},{1,3},{2,0},{3,1},{4,6},{5,7},{6,4},{7,5},{8,10},{9,11},{10,... | collective-permute-start | bytes 393224 | tf_op jit(solution)/shard_map/ppermute | solution.py:418
  36.1 9.3 %collective-permute-start.8 = (bf16[512,128]{1,0:T(8,128)(2,1)}, bf16[512,128]{1,0:T(8,128)(2,1)S(1)}, u32[]{:S(2)}, u32[]{:S(2)}) collective-permute-start(bf16[512,128]{1,0:T(8,128)(2,1)} %get-tuple-element.48), channel_id=1, source_target_pairs={{0,3},{1,2},{2,1},{3,0},{4,7},{5,6},{6,5},{7,4},{8,11},{9,10},{10,... | collective-permute-start | bytes 393224 | tf_op jit(solution)/shard_map/ppermute | solution.py:418
  37.6 11.5 %copy-start.4 = (f32[512,128]{1,0:T(8,128)S(1)}, f32[512,128]{1,0:T(8,128)}, u32[]{:S(2)}) copy-start(f32[512,128]{1,0:T(8,128)} %get-tuple-element.53) | copy-start | bytes 786436
  39.6 17.2 %copy-start.1 = (f32[1024,128]{1,0:T(8,128)S(1)}, f32[1024,128]{1,0:T(8,128)}, u32[]{:S(2)}) copy-start(f32[1024,128]{1,0:T(8,128)} %get-tuple-element.39) | copy-start | bytes 1572868
  39.6 13.4 %collective-permute-start.2 = (bf16[1024,128]{1,0:T(8,128)(2,1)}, bf16[1024,128]{1,0:T(8,128)(2,1)S(1)}, u32[]{:S(2)}, u32[]{:S(2)}) collective-permute-start(bf16[1024,128]{1,0:T(8,128)(2,1)} %get-tuple-element.40), channel_id=1, source_target_pairs={{1,0},{3,2},{4,5},{6,7},{9,8},{11,10},{12,13},{14,15},{17,16},{19,... | collective-permute-start | bytes 786440 | tf_op jit(solution)/shard_map/ppermute | solution.py:418
  42.7 7.3 %copy-start.2 = (f32[256,256]{1,0:T(8,128)}, f32[256,256]{1,0:T(8,128)S(1)}, u32[]{:S(2)}) copy-start(f32[256,256]{1,0:T(8,128)S(1)} %collective-permute-done.9.refs_3_) | copy-start | bytes 786436
  45.5 4.5 %collective-permute-start.10 = (f32[256,256]{1,0:T(8,128)S(1)}, f32[256,256]{1,0:T(8,128)S(1)}, u32[]{:S(2)}, u32[]{:S(2)}) collective-permute-start(f32[256,256]{1,0:T(8,128)S(1)} %collective-permute-done.9.refs_3_), channel_id=1, source_target_pairs={{0,1},{1,0},{2,3},{3,2},{4,5},{5,4},{6,7},{7,6},{8,9},{9,8},{10,11... | collective-permute-start | bytes 786440 | tf_op jit(solution)/shard_map/ppermute | solution.py:418
  46.5 6.6 %collective-permute-start.3 = (bf16[1024,128]{1,0:T(8,128)(2,1)}, bf16[1024,128]{1,0:T(8,128)(2,1)S(1)}, u32[]{:S(2)}, u32[]{:S(2)}) collective-permute-start(bf16[1024,128]{1,0:T(8,128)(2,1)} %get-tuple-element.41), channel_id=1, source_target_pairs={{1,3},{3,1},{4,6},{6,4},{9,11},{11,9},{12,14},{14,12},{17,19},{19,... | collective-permute-start | bytes 786440 | tf_op jit(solution)/shard_map/ppermute | solution.py:418
  47.2 9.7 %collective-permute-start.4 = (bf16[1024,128]{1,0:T(8,128)(2,1)}, bf16[1024,128]{1,0:T(8,128)(2,1)S(1)}, u32[]{:S(2)}, u32[]{:S(2)}) collective-permute-start(bf16[1024,128]{1,0:T(8,128)(2,1)} %get-tuple-element.42), channel_id=1, source_target_pairs={{1,2},{3,0},{4,7},{6,5},{9,10},{11,8},{12,15},{14,13},{17,18},{19,... | collective-permute-start | bytes 786440 | tf_op jit(solution)/shard_map/ppermute | solution.py:418
  49.9 0.7 copy-start.3
  57.7 12.4 %collective-permute-start.12 = (bf16[512,128]{1,0:T(8,128)(2,1)}, bf16[512,128]{1,0:T(8,128)(2,1)}, u32[]{:S(2)}, u32[]{:S(2)}) collective-permute-start(bf16[512,128]{1,0:T(8,128)(2,1)} %get-tuple-element.64), channel_id=1, source_target_pairs={{0,8},{1,9},{2,10},{3,11},{4,12},{5,13},{6,14},{7,15},{8,16},{9,17... | collective-permute-start | bytes 393224 | tf_op jit(solution)/shard_map/ppermute | solution.py:418
  62.1 8.6 %collective-permute-start.13 = (bf16[512,128]{1,0:T(8,128)(2,1)}, bf16[512,128]{1,0:T(8,128)(2,1)}, u32[]{:S(2)}, u32[]{:S(2)}) collective-permute-start(bf16[512,128]{1,0:T(8,128)(2,1)} %get-tuple-element.65), channel_id=1, source_target_pairs={{0,8},{1,9},{2,10},{3,11},{8,16},{9,17},{10,18},{11,19},{16,24},{1... | collective-permute-start | bytes 393224 | tf_op jit(solution)/shard_map/ppermute | solution.py:418
  67.9 7.8 %collective-permute-start.14 = (bf16[512,128]{1,0:T(8,128)(2,1)}, bf16[512,128]{1,0:T(8,128)(2,1)}, u32[]{:S(2)}, u32[]{:S(2)}) collective-permute-start(bf16[512,128]{1,0:T(8,128)(2,1)} %get-tuple-element.66), channel_id=1, source_target_pairs={{0,4},{1,5},{2,6},{3,7},{4,0},{5,1},{6,2},{7,3},{8,12},{9,13},{10,... | collective-permute-start | bytes 393224 | tf_op jit(solution)/shard_map/ppermute | solution.py:418
  68.2 9.7 %collective-permute-start.11 = (bf16[256,256]{1,0:T(8,128)(2,1)}, bf16[256,256]{1,0:T(8,128)(2,1)}, u32[]{:S(2)}, u32[]{:S(2)}) collective-permute-start(bf16[256,256]{1,0:T(8,128)(2,1)} %get-tuple-element.62), channel_id=1, source_target_pairs={{0,2},{1,3},{2,0},{3,1},{4,6},{5,7},{6,4},{7,5},{8,10},{9,11},{10,... | collective-permute-start | bytes 393224 | tf_op jit(solution)/shard_map/ppermute | solution.py:418
